TPU v7x, 32 devices: a whole 2x2x4 slice. The times are simulated.
32 devices in a mesh: front: 16 (over z, y, x), panel: 2 (over core).
Axes of the slice: x: 2, y: 2, z: 4, core: 2. Of those that a mesh axis runs over, the one named last changes fastest.
Arguments:
- sep_factor: bfloat16 [16384, 1024], P(('front', 'panel')), may hold values from -3 to 3, as said below
- coup_factor: bfloat16 [32768, 1024], P(('front', 'panel')), may hold values from -0.1875 to 0.1875
- coup_list: int32 [16, 16], replicated, may hold values from -1 to 15, as said below
- slot_tiles: int32 [16, 16], replicated, may hold values from 0 to 255, as said below
- anc_tiles: bfloat16 [32768, 128], P('front'), may hold values from -50 to 50
Outputs:
- selected_inverse: float32 [16384, 1024], P(('front', 'panel'))
- variances: float32 [16384], P(('front', 'panel'))
Inputs may be any that keep to these rules, and one draw needn't show every extreme that they name: `sep_factor`: each front's block of 1024 rows is lower triangular with a diagonal of 1 or more. `coup_list`: a front's entries name distinct blocks; live entries come first and the rest are -1; every front has 4 or more live entries and some front has 16. `slot_tiles`: every strip id of 0 to 255 appears in exactly one slot; every group holds exactly one strip of each block row.
All inputs are finite; a program needn't handle non-finite values.
Results may differ from a plain program's by a relative error of at most 0.0056.
Values may be sent and summed in bfloat16 or wider, within the bound.
A program may use at most 128 MiB of HBM per device.

v0:
```python
import functools

import jax
import jax.numpy as jnp
from jax import lax
from jax.experimental import pallas as pl
from jax.experimental.pallas import tpu as pltpu
from jax.sharding import PartitionSpec as P

BF = jnp.bfloat16
F32 = jnp.float32
DIAG = 128
MESH = pl.DeviceIdType.MESH


def mm(a, b):
    return jnp.dot(a, b, preferred_element_type=F32)


def split(x):
    hi = x.astype(BF)
    return hi, (x - hi.astype(F32)).astype(BF)


def flip(index, mask):
    bit = 1
    while bit <= mask:
        if mask & bit:
            index = index + bit * (1 - 2 * ((index // bit) % 2))
        bit *= 2
    return index


def first_kernel(
    depth,
    sep_ref,
    coup_ref,
    anc_ref,
    wide_out,
    wide_other,
    square_out,
    pool_ref,
    inv_ref,
    wide_ref,
    square_ref,
    lmat,
    coup_all,
    xl,
    xd,
    panel_send,
    panel_recv,
    z_recv,
    x_recv,
    y_recv,
    first_recv,
    second_recv,
    share_recv,
    out_send,
    local_sem,
):
    me = lax.axis_index("panel")
    group = lax.axis_index("front")
    layer, spot = group // 4, group % 4
    half, n = sep_ref.shape[0], sep_ref.shape[1]
    slab = anc_ref.shape[0]
    part = slab // 2
    partner = (group, 1 - me)
    beside = (layer * 4 + flip(spot, 1), me)
    behind = (layer * 4 + flip(spot, 2), me)
    peers = [(flip(layer, k) * 4 + spot, me) for k in range(1, depth)]

    barrier = pltpu.get_barrier_semaphore()
    for device in [partner, beside, behind] + peers:
        pl.semaphore_signal(barrier, inc=1, device_id=device, device_id_type=MESH)
    pl.semaphore_wait(barrier, 2 + depth)

    def remote(source, target, send, recv, device):
        return pltpu.make_async_remote_copy(
            src_ref=source, dst_ref=target, send_sem=send, recv_sem=recv, device_id=device, device_id_type=MESH
        )

    def place(k, mask, low=0, size=part):
        owner = flip(layer, k) * 4 + flip(spot, mask)
        start = pl.multiple_of(owner * slab + me * part + low, part // 2)
        return pool_ref.at[pl.ds(start, size), :]

    def push(source, target, recv, device):
        remote(source, target, out_send, recv, device).start()

    def arrived(target, recv):
        remote(target, target, out_send, recv, partner).wait_recv()

    own = anc_ref.at[pl.ds(pl.multiple_of(me * part, part), part), :]

    def open_block(k):
        source = own if k == 0 else place(k, 0)
        if k > 0:
            arrived(source, z_recv.at[k])
        piece = part // 2
        for first in (True, False):
            for recv, device, low in (
                (x_recv, beside, piece if first else 0),
                (y_recv, behind, 0 if first else piece),
            ):
                push(
                    source.at[pl.ds(low, piece), :],
                    place(k, 0, low, piece),
                    recv.at[k if first else depth + k],
                    device,
                )
        if k > 0:
            push(source, source, share_recv, partner)

    def relay(k):
        piece = part // 2
        arrived(place(k, 1, piece, piece), x_recv.at[k])
        push(place(k, 1, piece, piece), place(k, 1, piece, piece), second_recv.at[k], behind)
        arrived(place(k, 2, 0, piece), y_recv.at[k])
        push(place(k, 2, 0, piece), place(k, 2, 0, piece), first_recv.at[k], beside)
        arrived(place(k, 1, 0, piece), x_recv.at[depth + k])
        arrived(place(k, 2, piece, piece), y_recv.at[depth + k])
        push(place(k, 1), place(k, 1), share_recv, partner)
        push(place(k, 2), place(k, 2), share_recv, partner)

    def finish(k):
        piece = part // 2
        arrived(place(k, 3, 0, piece), first_recv.at[k])
        arrived(place(k, 3, piece, piece), second_recv.at[k])
        push(place(k, 3), place(k, 3), share_recv, partner)

    def stage(k):
        if 2 <= k <= depth + 1:
            finish(k - 2)
        if 1 <= k <= depth:
            relay(k - 1)
        if k < depth:
            open_block(k)

    rows = coup_ref.shape[0]
    upper = pl.ds(pl.multiple_of(me * half, half), half)
    sep_copy = remote(sep_ref, lmat.at[upper, :], panel_send.at[0], panel_recv.at[0], partner)
    coup_copy = remote(coup_ref, coup_all.at[pl.ds(rows, rows), :], panel_send.at[1], panel_recv.at[1], partner)
    wide_copy = remote(wide_ref, wide_other, panel_send.at[2], panel_recv.at[2], partner)
    sep_keep = pltpu.make_async_copy(sep_ref, lmat.at[upper, :], local_sem.at[0])
    sep_copy.start()
    for k in range(1, depth):
        push(own, place(0, 0), z_recv.at[k], peers[k - 1])
        if k == 1:
            stage(0)
    coup_copy.start()
    sep_keep.start()
    coup_keep = pltpu.make_async_copy(coup_ref, coup_all.at[pl.ds(0, rows), :], local_sem.at[1])
    coup_keep.start()
    keep = pltpu.make_async_copy(
        anc_ref, pool_ref.at[pl.ds(pl.multiple_of(group * slab, slab), slab), :], local_sem.at[2]
    )
    keep.start()

    inv_ref[...] = jnp.zeros_like(inv_ref)
    xl[...] = jnp.zeros_like(xl)
    sep_keep.wait()
    remote(sep_ref, lmat.at[pl.ds(pl.multiple_of((1 - me) * half, half), half), :], panel_send.at[0], panel_recv.at[0], partner).wait_recv()

    blocks = n // DIAG
    row = lax.broadcasted_iota(jnp.int32, (DIAG, DIAG), 0)
    col = lax.broadcasted_iota(jnp.int32, (DIAG, DIAG), 1)
    eye = row == col
    for b in range(blocks):
        span = pl.ds(b * DIAG, DIAG)
        block = lmat[span, span].astype(F32)
        xd[b] = jnp.where(eye, 1.0 / jnp.where(eye, block, 1.0), 0.0)

    def level(step, carry):
        mask = (
            ((row >> (step + 1)) == (col >> (step + 1)))
            & (((row >> step) & 1) == 1)
            & (((col >> step) & 1) == 0)
        )
        for b in range(blocks):
            span = pl.ds(b * DIAG, DIAG)
            x = xd[b]
            hi, lo = split(x)
            below = jnp.where(mask, lmat[span, span].astype(F32), 0.0).astype(BF)
            y = mm(below, jnp.concatenate([hi, lo], axis=1))
            yhi, ylo = split(y[:, :DIAG] + y[:, DIAG:])
            t = mm(jnp.concatenate([hi, lo], axis=0), jnp.concatenate([yhi, ylo], axis=1))
            t = (t[:DIAG, :DIAG] + t[:DIAG, DIAG:]) + (t[DIAG:, :DIAG] + t[DIAG:, DIAG:])
            xd[b] = x - t
        return carry

    levels = DIAG.bit_length() - 1
    lax.fori_loop(0, levels // 2, level, 0)
    stage(1)
    lax.fori_loop(levels // 2, levels, level, 0)
    for b in range(blocks):
        span = pl.ds(b * DIAG, DIAG)
        inv_ref[span, span], xl[span, span] = split(xd[b])
    size = DIAG
    while size < n:
        for start in range(0, n, 2 * size):
            top, low = pl.ds(start, size), pl.ds(start + size, size)
            below = lmat[low, top]
            thi, tlo = split(mm(below, inv_ref[top, top]) + mm(below, xl[top, top]))
            t = mm(inv_ref[low, low], thi) + (mm(inv_ref[low, low], tlo) + mm(xl[low, low], thi))
            inv_ref[low, top], xl[low, top] = split(-t)
        size *= 2
    stage(2)

    chunk = min(512, rows)
    columns = pl.ds(pl.multiple_of(me * half, half), half)
    coup_keep.wait()
    coup_copy.wait_recv()

    @pl.loop(0, 2 * rows // chunk)
    def _(i):
        take = pl.ds(pl.multiple_of(i * chunk, chunk), chunk)
        wide_ref[take, :] = mm(coup_all[take, :], inv_ref[:, columns]).astype(BF)

    stage(3)
    wide_copy.start()
    wide_keep = pltpu.make_async_copy(wide_ref, wide_out, local_sem.at[3])
    wide_keep.start()
    strip = pool_ref.shape[0] - 4 * depth * slab
    blank = pltpu.make_async_copy(
        inv_ref.at[pl.ds(0, strip), pl.ds(n - DIAG, DIAG)], pool_ref.at[pl.ds(4 * depth * slab, strip), :], local_sem.at[4]
    )
    blank.start()

    @pl.loop(0, n // 256)
    def _(i):
        take = pl.ds(pl.multiple_of(i * 256, 256), 256)
        square_ref[:, take] = lax.dot_general(
            inv_ref[:, columns], inv_ref[:, take], (((0,), (0,)), ((), ())), preferred_element_type=F32
        )

    square_keep = pltpu.make_async_copy(square_ref, square_out, local_sem.at[5])
    square_keep.start()
    for k in range(4, depth + 2):
        stage(k)

    total = 4 * depth - 1
    shared = pool_ref.at[pl.ds(0, total * part), :]
    remote(shared, shared, out_send, share_recv, partner).wait_recv()
    sent = pool_ref.at[pl.ds(0, (2 * total) * part), :]
    remote(sent, sent, out_send, share_recv, partner).wait_send()
    for copy in (keep, wide_keep, blank, square_keep):
        copy.wait()
    sep_copy.wait_send()
    coup_copy.wait_send()
    wide_copy.wait()


def last_kernel(
    list_ref,
    slot_ref,
    wide_in,
    other_in,
    square_in,
    pool_ref,
    out_ref,
    var_ref,
    sigma,
    wide,
    wide_other,
    carried,
    out,
    place,
    tile_sem,
    load_sem,
    store_sem,
):
    me = lax.axis_index("panel")
    group = lax.axis_index("front")
    rows, half = wide.shape
    edge = pool_ref.shape[1]
    groups, slots = slot_ref.shape
    total = groups * slots
    strip_rows = rows * rows // (total * edge)
    strip_count = edge // strip_rows
    across = rows // edge
    chunks = tile_sem.shape[0]
    chunk = rows // chunks
    low, high = pl.ds(0, rows // 2), pl.ds(rows // 2, rows // 2)

    load_wide = pltpu.make_async_copy(wide_in, wide, load_sem.at[0])
    load_low = pltpu.make_async_copy(other_in.at[high, :], wide_other.at[low, :], load_sem.at[1])
    load_high = pltpu.make_async_copy(other_in.at[low, :], wide_other.at[high, :], load_sem.at[2])
    load_square = pltpu.make_async_copy(square_in, out, load_sem.at[3])
    load_wide.start()

    @pl.loop(0, groups)
    def _(g):
        for s in range(slots):
            place[slot_ref[g, s]] = g * slots + s

    def block(i):
        return list_ref[group, (i + me * (across // 2)) % across]

    def fetch(i):
        a = block(i)
        for j in range(across):
            b = block(j)
            live = (a >= 0) & (b >= 0)
            for q in range(strip_count):
                at = place[jnp.where(live, a * groups + b * strip_count + q, 0)]
                source = pl.multiple_of(jnp.where(live, at, total) * strip_rows, strip_rows)
                down = pl.multiple_of(i * edge + q * strip_rows, strip_rows)
                pltpu.make_async_copy(
                    pool_ref.at[pl.ds(source, strip_rows), :],
                    sigma.at[pl.ds(down, strip_rows), pl.ds(j * edge, edge)],
                    tile_sem.at[i // (across // chunks)],
                ).start()

    pl.loop(0, across)(fetch)
    load_low.start()
    load_high.start()
    load_square.start()
    load_wide.wait()

    @pl.loop(0, chunks)
    def _(i):
        take = pl.ds(pl.multiple_of(i * chunk, chunk), chunk)
        pltpu.make_async_copy(sigma.at[take, :], sigma.at[take, :], tile_sem.at[i]).wait()
        carried[:, take] = mm(sigma[take, :], wide[...]).T.astype(BF)

    load_low.wait()
    load_high.wait()
    load_square.wait()
    step = 256
    for source, base in ((wide, me), (wide_other, 1 - me)):
        for c in range(half // step):
            put = pl.ds(pl.multiple_of(base * half + c * step, step), step)
            out[:, put] += mm(carried[...], source[:, pl.ds(c * step, step)])
            pltpu.make_async_copy(out.at[:, put], out_ref.at[:, put], store_sem).start()
    block_out = out[:, pl.ds(pl.multiple_of(me * half, half), half)]
    row = lax.broadcasted_iota(jnp.int32, (half, half), 0)
    col = lax.broadcasted_iota(jnp.int32, (half, half), 1)
    var_ref[...] = jnp.sum(jnp.where(row == col, block_out, 0.0), axis=0, keepdims=True)
    pltpu.make_async_copy(out, out_ref, store_sem).wait()


def on_device(sep_factor, coup_factor, coup_list, slot_tiles, anc_tiles):
    panels = lax.axis_size("panel")
    groups = lax.axis_size("front")
    half, width = sep_factor.shape
    edge = anc_tiles.shape[1]
    slots = slot_tiles.shape[1]
    strip_rows = anc_tiles.shape[0] // slots
    rows = coup_list.shape[1] * edge
    vmem = pl.BlockSpec(memory_space=pltpu.VMEM)
    smem = pl.BlockSpec(memory_space=pltpu.SMEM)
    hbm = pl.BlockSpec(memory_space=pltpu.HBM)
    depth = groups // 4
    dma = pltpu.SemaphoreType.DMA
    wide, wide_other, square, pool = pl.pallas_call(
        functools.partial(first_kernel, depth),
        out_shape=(
            jax.ShapeDtypeStruct((rows, half), BF),
            jax.ShapeDtypeStruct((rows, half), BF),
            jax.ShapeDtypeStruct((half, width), F32),
            jax.ShapeDtypeStruct((groups * anc_tiles.shape[0] + strip_rows, edge), BF),
        ),
        in_specs=[hbm] * 3,
        out_specs=[hbm] * 4,
        scratch_shapes=[
            pltpu.VMEM((width, width), BF),
            pltpu.VMEM((rows, half), BF),
            pltpu.VMEM((half, width), F32),
            pltpu.VMEM((width, width), BF),
            pltpu.VMEM((rows, width), BF),
            pltpu.VMEM((width, width), BF),
            pltpu.VMEM((width // DIAG, DIAG, DIAG), F32),
            dma((3,)),
            dma((3,)),
            dma((depth,)),
            dma((2 * depth,)),
            dma((2 * depth,)),
            dma((depth,)),
            dma((depth,)),
            dma,
            dma,
            dma((6,)),
        ],
        compiler_params=pltpu.CompilerParams(
            vmem_limit_bytes=63 << 20, collective_id=0, has_side_effects=True
        ),
    )(sep_factor, coup_factor, anc_tiles)
    selected, variances = pl.pallas_call(
        last_kernel,
        out_shape=(
            jax.ShapeDtypeStruct((half, width), F32),
            jax.ShapeDtypeStruct((1, half), F32),
        ),
        in_specs=[smem, smem] + [hbm] * 4,
        out_specs=[hbm, vmem],
        scratch_shapes=[
            pltpu.VMEM((rows, rows), BF),
            pltpu.VMEM((rows, half), BF),
            pltpu.VMEM((rows, half), BF),
            pltpu.VMEM((half, rows), BF),
            pltpu.VMEM((half, width), F32),
            pltpu.SMEM((groups * slots,), jnp.int32),
            dma((4,)),
            dma((4,)),
            dma,
        ],
        compiler_params=pltpu.CompilerParams(vmem_limit_bytes=63 << 20),
    )(coup_list, slot_tiles, wide, wide_other, square, pool)
    return selected, variances.reshape(half)


def solution(mesh):
    placed = (P(("front", "panel"), None), P(("front", "panel"), None), P(), P(), P("front", None))
    return jax.shard_map(
        on_device,
        mesh=mesh,
        in_specs=placed,
        out_specs=(P(("front", "panel"), None), P(("front", "panel"))),
        check_vma=False,
    )
```

profile of v0, /device:TPU:0, one launch (start us, length us, event | category | flops | bytes accessed | tf_op | source)
XLA Modules:
  0.0 65.8 jit_solution(8174122060149237447)
XLA Ops:
  0.6 48.6 %shard_map.68 = (bf16[2048,512]{1,0:T(8,128)(2,1)}, bf16[2048,512]{1,0:T(8,128)(2,1)}, f32[512,1024]{1,0:T(8,128)}, bf16[32896,128]{1,0:T(8,128)(2,1)}) custom-call(bf16[512,1024]{1,0:T(8,128)(2,1)} %sep_ref.1, bf16[1024,1024]{1,0:T(8,128)(2,1)} %coup_ref.1, bf16[2048,128]{1,0:T(8,128)(2,1)} %anc_ref.1), custom_call_target="tpu_custom_call" | custom-call | tf_op jit(solution)/shard_map/pallas_call | solution.py:355
  49.2 16.5 %shard_map.69 = (f32[512,1024]{1,0:T(8,128)}, f32[1,512]{1,0:T(1,128)}) custom-call(s32[16,16]{1,0:T(8,128)} %list_ref.1, s32[16,16]{1,0:T(8,128)} %slot_ref.1, bf16[2048,512]{1,0:T(8,128)(2,1)} %get-tuple-element.8.wide_in, bf16[2048,512]{1,0:T(8,128)(2,1)} %get-tuple-element.9.other_in, f32[512,1024]{1,0:T(8,128)} %get-tuple-element.10.square_in, ...), custom_call_target="tpu_custom_call" | custom-call | tf_op jit(solution)/shard_map/pallas_call | solution.py:388
where the time goes:
time: 65.9 us; the launch traced here: 65.8 us
  Pallas kernels  65.1 us (99%)
    pallas_call x1, Pallas kernels, on_device(): pl.pallas_call(functools.partial(first_kernel, depth), out_shape=(jax.Sha...  48.6 us
    pallas_call x1, Pallas kernels, on_device(): pl.pallas_call(last_kernel, out_shape=(jax.ShapeDtypeStruct((half, width)...  16.5 us

commit v1 on v0

--- a/solution.py
+++ b/solution.py
@@ -339,6 +339,352 @@
     pltpu.make_async_copy(out, out_ref, store_sem).wait()
 
 
+def gather_kernel(
+    depth,
+    slot_ref,
+    sep_ref,
+    coup_ref,
+    anc_ref,
+    pool,
+    wide,
+    turned,
+    out,
+    strips,
+    lmat,
+    coup,
+    inv_ref,
+    xl,
+    xd,
+    panel_send,
+    panel_recv,
+    z_recv,
+    x_recv,
+    y_recv,
+    first_recv,
+    second_recv,
+    share_recv,
+    out_send,
+    local_sem,
+):
+    me = lax.axis_index("panel")
+    group = lax.axis_index("front")
+    layer, spot = group // 4, group % 4
+    half, n = sep_ref.shape
+    groups, slots = slot_ref.shape
+    edge = anc_ref.shape[1]
+    side = edge // 2
+    rows = coup_ref.shape[0]
+    across = 2 * rows // edge
+    mine = slots // 2
+    body = mine * side
+    part = body + across
+    low_size = part // 32 * 16
+    low_size = part - low_size if part % 32 else low_size
+    partner = (group, 1 - me)
+    beside = (layer * 4 + flip(spot, 1), me)
+    behind = (layer * 4 + flip(spot, 2), me)
+    peers = [(flip(layer, k) * 4 + spot, me) for k in range(1, depth)]
+
+    strip_load = pltpu.make_async_copy(
+        anc_ref.at[pl.ds(pl.multiple_of(me * mine * edge, mine * edge), mine * edge), :], strips, local_sem.at[0]
+    )
+    strip_load.start()
+    upper = pl.ds(pl.multiple_of(me * half, half), half)
+    sep_keep = pltpu.make_async_copy(sep_ref, lmat.at[upper, :], local_sem.at[1])
+    sep_keep.start()
+    coup_keep = pltpu.make_async_copy(coup_ref, coup, local_sem.at[2])
+    coup_keep.start()
+
+    barrier = pltpu.get_barrier_semaphore()
+    for device in [partner, beside, behind] + peers:
+        pl.semaphore_signal(barrier, inc=1, device_id=device, device_id_type=MESH)
+
+    def remote(source, target, send, recv, device):
+        return pltpu.make_async_remote_copy(
+            src_ref=source, dst_ref=target, send_sem=send, recv_sem=recv, device_id=device, device_id_type=MESH
+        )
+
+    def place(k, mask, piece=None):
+        owner = flip(layer, k) * 4 + flip(spot, mask)
+        low, size = ((0, part), (0, low_size), (low_size, part - low_size))[0 if piece is None else piece + 1]
+        start = pl.multiple_of((owner * 2 + me) * part + low, 16)
+        return pool.at[pl.ds(start, size), :]
+
+    def push(source, recv, device):
+        remote(source, source, out_send, recv, device).start()
+
+    def arrived(target, recv):
+        remote(target, target, out_send, recv, partner).wait_recv()
+
+    def open_block(k):
+        if k > 0:
+            arrived(place(k, 0), z_recv.at[k])
+        for first in (True, False):
+            for recv, device, piece in ((x_recv, beside, 1 if first else 0), (y_recv, behind, 0 if first else 1)):
+                push(place(k, 0, piece), recv.at[k if first else depth + k], device)
+        push(place(k, 0), share_recv, partner)
+
+    def relay(k):
+        arrived(place(k, 1, 1), x_recv.at[k])
+        push(place(k, 1, 1), second_recv.at[k], behind)
+        arrived(place(k, 2, 0), y_recv.at[k])
+        push(place(k, 2, 0), first_recv.at[k], beside)
+
+    def collect(k):
+        arrived(place(k, 1, 0), x_recv.at[depth + k])
+        arrived(place(k, 2, 1), y_recv.at[depth + k])
+        push(place(k, 1), share_recv, partner)
+        push(place(k, 2), share_recv, partner)
+
+    def finish(k):
+        arrived(place(k, 3, 0), first_recv.at[k])
+        arrived(place(k, 3, 1), second_recv.at[k])
+        push(place(k, 3), share_recv, partner)
+
+    row = lax.broadcasted_iota(jnp.int32, (side, edge), 0)
+    lane = lax.broadcasted_iota(jnp.int32, (side, edge), 1)
+    left = lane < side
+    column = jnp.where(left, lane, lane - side)
+    left_flag = jnp.where(left, 1, 0)
+    triangle = jnp.where(column >= row, 1, 0)
+    list_row = lax.broadcasted_iota(jnp.int32, (across, edge), 0)
+    mine_at = pl.multiple_of((group * 2 + me) * part, 16)
+    strip_load.wait()
+    extra = jnp.zeros((across, edge), F32)
+    for s in range(mine):
+        tile_id = slot_ref[group, me * mine + s]
+        i, j = tile_id // across, tile_id % across
+        tile = strips[s * edge : (s + 1) * edge, :].astype(F32)
+        chosen = jnp.where(jnp.full((edge, edge), i - j) > 0, tile.T, tile)
+        top, bottom = chosen[:side, :], chosen[side:, :]
+        gap = jnp.full((side, edge), i - j)
+        wanted = jnp.where(gap == 0, triangle, jnp.where(gap < 0, 1, 0))
+        pool[pl.ds(mine_at + s * side, side), :] = jnp.where(left_flag == wanted, top, bottom).astype(BF)
+        line = jnp.sum(jnp.where(column == row, jnp.where(left, bottom, top), 0.0), axis=0, keepdims=True)
+        hit = jnp.where(jnp.full((across, edge), i - j) == 0, jnp.where(list_row == jnp.full((across, edge), i), 1, 0), 0)
+        extra = extra + jnp.where(hit == 1, line, 0.0)
+    pool[pl.ds(mine_at + body, across), :] = extra.astype(BF)
+
+    pl.semaphore_wait(barrier, 2 + depth)
+    sep_copy = remote(sep_ref, lmat.at[upper, :], panel_send.at[0], panel_recv.at[0], partner)
+    sep_copy.start()
+    for k in range(1, depth):
+        push(place(0, 0), z_recv.at[k], peers[k - 1])
+        if k == 1:
+            open_block(0)
+
+    inv_ref[...] = jnp.zeros_like(inv_ref)
+    xl[...] = jnp.zeros_like(xl)
+    wide[pl.ds(2 * rows, edge), :] = jnp.zeros((edge, n), BF)
+    turned[:, pl.ds(2 * rows, edge)] = jnp.zeros((half, edge), BF)
+    sep_keep.wait()
+    other = pl.ds(pl.multiple_of((1 - me) * half, half), half)
+    remote(sep_ref, lmat.at[other, :], panel_send.at[0], panel_recv.at[0], partner).wait_recv()
+
+    blocks = n // DIAG
+    row128 = lax.broadcasted_iota(jnp.int32, (DIAG, DIAG), 0)
+    col128 = lax.broadcasted_iota(jnp.int32, (DIAG, DIAG), 1)
+    eye = row128 == col128
+    for b in range(blocks):
+        span = pl.ds(b * DIAG, DIAG)
+        block = lmat[span, span].astype(F32)
+        xd[b] = jnp.where(eye, 1.0 / jnp.where(eye, block, 1.0), 0.0)
+
+    def level(step, carry):
+        mask = (
+            ((row128 >> (step + 1)) == (col128 >> (step + 1)))
+            & (((row128 >> step) & 1) == 1)
+            & (((col128 >> step) & 1) == 0)
+        )
+        for b in range(blocks):
+            span = pl.ds(b * DIAG, DIAG)
+            x = xd[b]
+            hi, lo = split(x)
+            below = jnp.where(mask, lmat[span, span].astype(F32), 0.0).astype(BF)
+            y = mm(below, jnp.concatenate([hi, lo], axis=1))
+            yhi, ylo = split(y[:, :DIAG] + y[:, DIAG:])
+            t = mm(jnp.concatenate([hi, lo], axis=0), jnp.concatenate([yhi, ylo], axis=1))
+            t = (t[:DIAG, :DIAG] + t[:DIAG, DIAG:]) + (t[DIAG:, :DIAG] + t[DIAG:, DIAG:])
+            xd[b] = x - t
+        return carry
+
+    def merge(size):
+        for start in range(0, n, 2 * size):
+            top, low = pl.ds(start, size), pl.ds(start + size, size)
+            below = lmat[low, top]
+            thi, tlo = split(mm(below, inv_ref[top, top]) + mm(below, xl[top, top]))
+            t = mm(inv_ref[low, low], thi) + (mm(inv_ref[low, low], tlo) + mm(xl[low, low], thi))
+            inv_ref[low, top], xl[low, top] = split(-t)
+
+    levels = DIAG.bit_length() - 1
+    lax.fori_loop(0, levels // 2, level, 0)
+    relay(0)
+    open_block(1)
+    collect(0)
+    lax.fori_loop(levels // 2, levels, level, 0)
+    for b in range(blocks):
+        span = pl.ds(b * DIAG, DIAG)
+        inv_ref[span, span], xl[span, span] = split(xd[b])
+    relay(1)
+    merge(DIAG)
+    open_block(2)
+    finish(0)
+    collect(1)
+    size = 2 * DIAG
+    while size < n:
+        merge(size)
+        size *= 2
+    relay(2)
+    coup_keep.wait()
+    own_rows = pl.ds(pl.multiple_of(me * rows, rows), rows)
+    step = 256
+    for c in range(n // step):
+        put = pl.ds(c * step, step)
+        deep = pl.ds(c * step, n - c * step)
+        wide[own_rows, put] = mm(coup[:, deep], inv_ref[deep, put]).astype(BF)
+    open_block(3)
+    finish(1)
+    collect(2)
+    wide_copy = remote(wide.at[own_rows, :], wide.at[own_rows, :], panel_send.at[1], panel_recv.at[1], partner)
+    wide_copy.start()
+    columns = pl.ds(pl.multiple_of(me * half, half), half)
+
+    @pl.loop(0, n // step)
+    def _(i):
+        take = pl.ds(pl.multiple_of(i * step, step), step)
+        out[:, take] = lax.dot_general(
+            inv_ref[:, columns], inv_ref[:, take], (((0,), (0,)), ((), ())), preferred_element_type=F32
+        )
+
+    relay(3)
+    finish(2)
+    other_rows = pl.ds(pl.multiple_of((1 - me) * rows, rows), rows)
+    remote(wide.at[other_rows, :], wide.at[other_rows, :], panel_send.at[1], panel_recv.at[1], partner).wait_recv()
+
+    @pl.loop(0, across)
+    def _(c):
+        put = pl.ds(pl.multiple_of(c * edge, edge), edge)
+        turned[:, put] = wide[put, columns].T
+
+    collect(3)
+    finish(3)
+    total = 4 * depth
+    shared = pool.at[pl.ds(0, total * part), :]
+    remote(shared, shared, out_send, share_recv, partner).wait_recv()
+
+    sent = pool.at[pl.ds(0, (2 * total - 1) * part), :]
+    remote(sent, sent, out_send, share_recv, partner).wait_send()
+    sep_copy.wait_send()
+    wide_copy.wait_send()
+
+
+def select_kernel(
+    list_ref,
+    slot_ref,
+    pool,
+    wide,
+    flat,
+    square,
+    out_ref,
+    var_ref,
+    table,
+    natural,
+    turned,
+    sigma,
+    carried,
+    out,
+    load_sem,
+    store_sem,
+):
+    me = lax.axis_index("panel")
+    group = lax.axis_index("front")
+    groups, slots = slot_ref.shape
+    edge = pool.shape[1]
+    side = edge // 2
+    half, n = out.shape
+    across = sigma.shape[0] // edge
+    rows = sigma.shape[0] // 2
+    mine = slots // 2
+    body = mine * side
+    part = body + across
+    step = 256
+    columns = pl.ds(pl.multiple_of(me * half, half), half)
+
+    for c in range(across):
+        at = across
+        for a in range(across):
+            at = jnp.where(list_ref[group, a] == c, a, at)
+        source = pl.ds(pl.multiple_of(at * edge, edge), edge)
+        put = pl.ds(c * edge, edge)
+        pltpu.make_async_copy(flat.at[:, source], turned.at[:, put], load_sem.at[0]).start()
+        pltpu.make_async_copy(wide.at[source, :], natural.at[put, :], load_sem.at[1]).start()
+
+    @pl.loop(0, groups)
+    def _(g):
+        for s in range(slots):
+            table[slot_ref[g, s]] = (g * 2 + s // mine) * part + (s % mine) * side
+
+    row = lax.broadcasted_iota(jnp.int32, (side, edge), 0)
+    lane = lax.broadcasted_iota(jnp.int32, (side, edge), 1)
+    left = lane < side
+    column = jnp.where(left, lane, lane - side)
+
+    def packed(i, j):
+        tile_id = i * across + j
+        return pool[pl.ds(pl.multiple_of(table[tile_id], 16), side), :]
+
+    def span_of(i):
+        return pl.ds(pl.multiple_of(i * edge, edge), edge)
+
+    extra = jnp.zeros((across, edge), F32)
+    for g in range(2 * groups):
+        extra = extra + pool[g * part + body : g * part + part, :].astype(F32)
+
+    for i in range(across):
+        p = packed(i, i).astype(F32)
+        turn = jnp.concatenate([p, p], axis=0).T
+        d = jnp.broadcast_to(extra[i : i + 1, :], (side, edge))
+        keep, below, equal = column >= row, column < row, column == row
+        top = jnp.where(left, jnp.where(keep, p, turn[:side]), jnp.where(below, p, jnp.where(equal, d, turn[:side])))
+        bottom = jnp.where(left, jnp.where(below, p, jnp.where(equal, d, turn[side:])), jnp.where(keep, p, turn[side:]))
+        sigma[i * edge : (i + 1) * edge, i * edge : (i + 1) * edge] = jnp.concatenate([top, bottom], axis=0).astype(BF)
+
+    @pl.loop(0, across)
+    def _(i):
+        for d in range(1, across // 2 + 1):
+            other = (i + d) % across
+            a, b = jnp.minimum(i, other), jnp.maximum(i, other)
+            p, q = packed(a, b), packed(b, a)
+            sigma[span_of(a), span_of(b)] = jnp.concatenate([jnp.where(left, p, q), jnp.where(left, q, p)], axis=0)
+
+    for i in range(0, across, 2):
+        a, b = slice(i * edge, (i + 1) * edge), slice((i + 1) * edge, (i + 2) * edge)
+        sigma[b, a] = sigma[a, b].astype(F32).T.astype(BF)
+
+    pltpu.make_async_copy(turned, turned, load_sem.at[0]).wait()
+    size = 2 * rows
+    for c in range(size // step):
+        put = slice(c * step, (c + 1) * step)
+        end = (c + 1) * step
+        value = mm(turned[:, :end], sigma[:end, put])
+        if end < size:
+            value = value + lax.dot_general(
+                turned[:, end:], sigma[put, end:], (((1,), (1,)), ((), ())), preferred_element_type=F32
+            )
+        carried[:, put] = value.astype(BF)
+
+    pltpu.make_async_copy(natural, natural, load_sem.at[1]).wait()
+    for c in range(n // step):
+        put = slice(c * step, (c + 1) * step)
+        out[:, put] = square[:, put] + mm(carried[...], natural[:, put])
+        pltpu.make_async_copy(out.at[:, put], out_ref.at[:, put], store_sem).start()
+    block_out = out[:, columns]
+    row_out = lax.broadcasted_iota(jnp.int32, (half, half), 0)
+    col_out = lax.broadcasted_iota(jnp.int32, (half, half), 1)
+    var_ref[...] = jnp.sum(jnp.where(row_out == col_out, block_out, 0.0), axis=0, keepdims=True)
+    pltpu.make_async_copy(out, out_ref, store_sem).wait()
+
+
 def on_device(sep_factor, coup_factor, coup_list, slot_tiles, anc_tiles):
     panels = lax.axis_size("panel")
     groups = lax.axis_size("front")
@@ -352,6 +698,61 @@
     hbm = pl.BlockSpec(memory_space=pltpu.HBM)
     depth = groups // 4
     dma = pltpu.SemaphoreType.DMA
+    if strip_rows == edge:
+        part = slots // 2 * (edge // 2) + rows // edge
+        pool, wide, turned, square = pl.pallas_call(
+            functools.partial(gather_kernel, depth),
+            out_shape=(
+                pltpu.VMEM((2 * groups * part, edge), BF),
+                pltpu.VMEM((rows + edge, width), BF),
+                pltpu.VMEM((half, rows + edge), BF),
+                pltpu.VMEM((half, width), F32),
+            ),
+            in_specs=[smem] + [hbm] * 3,
+            out_specs=[vmem] * 4,
+            scratch_shapes=[
+                pltpu.VMEM((slots // 2 * edge, edge), BF),
+                pltpu.VMEM((width, width), BF),
+                pltpu.VMEM((rows // 2, width), BF),
+                pltpu.VMEM((width, width), BF),
+                pltpu.VMEM((width, width), BF),
+                pltpu.VMEM((width // DIAG, DIAG, DIAG), F32),
+                dma((2,)),
+                dma((2,)),
+                dma((depth,)),
+                dma((2 * depth,)),
+                dma((2 * depth,)),
+                dma((depth,)),
+                dma((depth,)),
+                dma,
+                dma,
+                dma((3,)),
+            ],
+            compiler_params=pltpu.CompilerParams(
+                vmem_limit_bytes=50 << 20, collective_id=0, has_side_effects=True
+            ),
+        )(slot_tiles, sep_factor, coup_factor, anc_tiles)
+        selected, variances = pl.pallas_call(
+            select_kernel,
+            out_shape=(
+                jax.ShapeDtypeStruct((half, width), F32),
+                jax.ShapeDtypeStruct((1, half), F32),
+            ),
+            in_specs=[smem, smem] + [vmem] * 4,
+            out_specs=[hbm, vmem],
+            scratch_shapes=[
+                pltpu.SMEM((groups * slots,), jnp.int32),
+                pltpu.VMEM((rows, width), BF),
+                pltpu.VMEM((half, rows), BF),
+                pltpu.VMEM((rows, rows), BF),
+                pltpu.VMEM((half, rows), BF),
+                pltpu.VMEM((half, width), F32),
+                dma((2,)),
+                dma,
+            ],
+            compiler_params=pltpu.CompilerParams(vmem_limit_bytes=50 << 20),
+        )(coup_list, slot_tiles, pool, wide, turned, square)
+        return selected, variances.reshape(half)
     wide, wide_other, square, pool = pl.pallas_call(
         functools.partial(first_kernel, depth),
         out_shape=(

time: 65.9 us -> 56.2 us (0.85)
  Pallas kernels: 65.1 us -> 49.8 us
  local copies, waits for them, and re-layouts: 0 us -> 5.51 us
    pallas_call x2, Pallas kernels: 65.1 us -> 49.8 us  [the longest x1 33.3 us: on_device(): pl.pallas_call(functools.partial(gather_kernel, depth), out_shape=(pltpu....]
    unnamed x0 -> x10, local copies, waits for them, and re-layouts: none -> 5.51 us
where the time goes in v1:
time: 56.2 us; the launch traced here: 55.9 us
  Pallas kernels  49.8 us (89%)
  local copies, waits for them, and re-layouts  5.51 us (10%)
  between operations  0.67 us (1%)
    pallas_call x1, Pallas kernels, on_device(): pl.pallas_call(functools.partial(gather_kernel, depth), out_shape=(pltpu....  33.3 us
    pallas_call x1, Pallas kernels, on_device(): pl.pallas_call(select_kernel, out_shape=(jax.ShapeDtypeStruct((half, widt...  16.4 us
    unnamed x10, local copies, waits for them, and re-layouts  5.51 us

profile of v1, /device:TPU:0, one launch (start us, length us, event | category | flops | bytes accessed | tf_op | source)
XLA Modules:
  0.0 55.9 jit_solution(14337513353086717029)
XLA Ops:
  0.6 0.0 copy-start.3
  0.6 0.0 copy-start.4
  0.7 33.3 %shard_map.68 = (bf16[16896,128]{1,0:T(8,128)(2,1)S(1)}, bf16[2176,1024]{1,0:T(8,128)(2,1)S(1)}, bf16[512,2176]{1,0:T(8,128)(2,1)S(1)}, f32[512,1024]{1,0:T(8,128)S(1)}) custom-call(s32[16,16]{1,0:T(8,128)} %slot_ref.3, bf16[512,1024]{1,0:T(8,128)(2,1)} %sep_ref.1, bf16[1024,1024]{1,0:T(8,128)(2,1)} %coup_ref.1, bf16[2048,128]{1,0:T(8,128)(2,1)} %anc_ref.1), custom_call_target="tpu_custom_call" | custom-call | tf_op jit(solution)/shard_map/pallas_call | solution.py:703
  34.0 0.0 copy-start
  34.0 2.0 %copy-done = bf16[2176,1024]{1,0:T(8,128)(2,1)} copy-done((bf16[2176,1024]{1,0:T(8,128)(2,1)}, bf16[2176,1024]{1,0:T(8,128)(2,1)S(1)}, u32[]{:S(2)}) %copy-start) | copy-done | bytes 4456472
  36.0 0.0 copy-start.1
  36.0 2.1 %copy-done.1 = bf16[16896,128]{1,0:T(8,128)(2,1)} copy-done((bf16[16896,128]{1,0:T(8,128)(2,1)}, bf16[16896,128]{1,0:T(8,128)(2,1)S(1)}, u32[]{:S(2)}) %copy-start.1) | copy-done | bytes 4325400
  38.1 0.0 copy-start.2
  38.1 1.4 %copy-done.2 = bf16[512,2176]{1,0:T(8,128)(2,1)} copy-done((bf16[512,2176]{1,0:T(8,128)(2,1)}, bf16[512,2176]{1,0:T(8,128)(2,1)S(1)}, u32[]{:S(2)}) %copy-start.2) | copy-done | bytes 2228248
  39.5 0.0 copy-done.3
  39.5 0.0 copy-done.4
  39.5 16.4 %shard_map.69 = (f32[512,1024]{1,0:T(8,128)}, f32[1,512]{1,0:T(1,128)}) custom-call(s32[16,16]{1,0:T(8,128)S(1)} %copy-done.4, s32[16,16]{1,0:T(8,128)S(1)} %copy-done.3, bf16[16896,128]{1,0:T(8,128)(2,1)} %copy-done.1, bf16[2176,1024]{1,0:T(8,128)(2,1)} %copy-done, bf16[512,2176]{1,0:T(8,128)(2,1)} %copy-done.2, f32[512,1024]{1,0:T(8,128)S(1)} %get-tuple-element.11.square), custom_call_target="tpu_custom_call" | custom-call | tf_op jit(solution)/shard_map/pallas_call | solution.py:735
Async XLA Ops:
  0.6 38.9 %copy-start.3 = (s32[16,16]{1,0:T(8,128)S(1)}, s32[16,16]{1,0:T(8,128)}, u32[]{:S(2)}) copy-start(s32[16,16]{1,0:T(8,128)} %slot_ref.3) | copy-start | bytes 3076
  0.6 38.9 %copy-start.4 = (s32[16,16]{1,0:T(8,128)S(1)}, s32[16,16]{1,0:T(8,128)}, u32[]{:S(2)}) copy-start(s32[16,16]{1,0:T(8,128)} %list_ref.1) | copy-start | bytes 3076
  34.0 2.0 %copy-start = (bf16[2176,1024]{1,0:T(8,128)(2,1)}, bf16[2176,1024]{1,0:T(8,128)(2,1)S(1)}, u32[]{:S(2)}) copy-start(bf16[2176,1024]{1,0:T(8,128)(2,1)S(1)} %get-tuple-element.9.wide) | copy-start | bytes 13369348
  36.0 2.1 %copy-start.1 = (bf16[16896,128]{1,0:T(8,128)(2,1)}, bf16[16896,128]{1,0:T(8,128)(2,1)S(1)}, u32[]{:S(2)}) copy-start(bf16[16896,128]{1,0:T(8,128)(2,1)S(1)} %get-tuple-element.8.pool) | copy-start | bytes 12976132
  38.1 1.4 %copy-start.2 = (bf16[512,2176]{1,0:T(8,128)(2,1)}, bf16[512,2176]{1,0:T(8,128)(2,1)S(1)}, u32[]{:S(2)}) copy-start(bf16[512,2176]{1,0:T(8,128)(2,1)S(1)} %get-tuple-element.10.flat) | copy-start | bytes 6684676

commit v2 on v1

--- a/solution.py
+++ b/solution.py
@@ -750,7 +750,7 @@
                 dma((2,)),
                 dma,
             ],
-            compiler_params=pltpu.CompilerParams(vmem_limit_bytes=50 << 20),
+            compiler_params=pltpu.CompilerParams(vmem_limit_bytes=36 << 20),
         )(coup_list, slot_tiles, pool, wide, turned, square)
         return selected, variances.reshape(half)
     wide, wide_other, square, pool = pl.pallas_call(

time: 56.2 us -> 47.2 us (0.84)
  local copies, waits for them, and re-layouts: 5.51 us -> 0.01 us
  Pallas kernels: 49.8 us -> 46.3 us
    unnamed x10 -> x4, local copies, waits for them, and re-layouts: 5.51 us -> 0.01 us
    pallas_call x1, Pallas kernels: 16.4 us -> 12.9 us  [on_device(): pl.pallas_call(select_kernel, out_shape=(jax.ShapeDtypeStruct((half, widt...]
where the time goes in v2:
time: 47.2 us; the launch traced here: 46.9 us
  Pallas kernels  46.3 us (98%)
  between operations  0.67 us (1%)
    pallas_call x1, Pallas kernels, on_device(): pl.pallas_call(functools.partial(gather_kernel, depth), out_shape=(pltpu....  33.3 us
    pallas_call x1, Pallas kernels, on_device(): pl.pallas_call(select_kernel, out_shape=(jax.ShapeDtypeStruct((half, widt...  12.9 us

profile of v2, /device:TPU:0, one launch (start us, length us, event | category | flops | bytes accessed | tf_op | source)
XLA Modules:
  0.0 46.9 jit_solution(1103239200156366170)
XLA Ops:
  0.6 0.0 copy-start
  0.6 0.0 copy-start.1
  0.7 33.3 %shard_map.68 = (bf16[16896,128]{1,0:T(8,128)(2,1)S(1)}, bf16[2176,1024]{1,0:T(8,128)(2,1)S(1)}, bf16[512,2176]{1,0:T(8,128)(2,1)S(1)}, f32[512,1024]{1,0:T(8,128)S(1)}) custom-call(s32[16,16]{1,0:T(8,128)} %slot_ref.3, bf16[512,1024]{1,0:T(8,128)(2,1)} %sep_ref.1, bf16[1024,1024]{1,0:T(8,128)(2,1)} %coup_ref.1, bf16[2048,128]{1,0:T(8,128)(2,1)} %anc_ref.1), custom_call_target="tpu_custom_call" | custom-call | tf_op jit(solution)/shard_map/pallas_call | solution.py:703
  34.0 0.0 copy-done
  34.0 0.0 copy-done.1
  34.0 12.9 %shard_map.69 = (f32[512,1024]{1,0:T(8,128)}, f32[1,512]{1,0:T(1,128)}) custom-call(s32[16,16]{1,0:T(8,128)S(1)} %copy-done.1, s32[16,16]{1,0:T(8,128)S(1)} %copy-done, bf16[16896,128]{1,0:T(8,128)(2,1)S(1)} %get-tuple-element.8.pool, bf16[2176,1024]{1,0:T(8,128)(2,1)S(1)} %get-tuple-element.9.wide, bf16[512,2176]{1,0:T(8,128)(2,1)S(1)} %get-tuple-element.10.flat, ...), custom_call_target="tpu_custom_call" | custom-call | tf_op jit(solution)/shard_map/pallas_call | solution.py:735
Async XLA Ops:
  0.6 33.4 %copy-start = (s32[16,16]{1,0:T(8,128)S(1)}, s32[16,16]{1,0:T(8,128)}, u32[]{:S(2)}) copy-start(s32[16,16]{1,0:T(8,128)} %slot_ref.3) | copy-start | bytes 3076
  0.6 33.4 %copy-start.1 = (s32[16,16]{1,0:T(8,128)S(1)}, s32[16,16]{1,0:T(8,128)}, u32[]{:S(2)}) copy-start(s32[16,16]{1,0:T(8,128)} %list_ref.1) | copy-start | bytes 3076
